TPU v7x, 512 devices: a whole 4x8x8 slice. The times are simulated.
512 devices in a mesh: group: 16 (over x, z_hi), shard: 32 (over y, z_lo, core).
Axes of the slice: x: 4, y: 8, z: 8 (z_hi: 4, z_lo: 2; z = z_hi * 2 + z_lo), core: 2. Of those that a mesh axis runs over, the one named last changes fastest.
Arguments:
- tokens: bfloat16 [32768, 2048], P(('group', 'shard')), may hold values from -7 to 7
- w_qk: bfloat16 [2048, 1024], P('shard'), may hold values from -0.09375 to 0.09375
- w_in: bfloat16 [128, 2048], replicated, may hold values from -0.5 to 0.5
- w_out: bfloat16 [2048, 128], replicated, may hold values from -0.125 to 0.125
- particles: bfloat16 [2097152, 128], P(('group', 'shard')), may hold values from -6 to 6
- cotangent: bfloat16 [2097152, 128], P(('group', 'shard')), may hold values from -6 to 6
- clusters: int32 [2097152], P(('group', 'shard')), may hold values from 0 to 63
- owners: int32 [16384], P(('group', 'shard')), may hold values from 0 to 31, as said below
Outputs:
- particle_out: bfloat16 [2097152, 128], P(('group', 'shard'))
- qk_grad: float32 [2048, 1024], P('shard')
Inputs may be any that keep to these rules, and one draw needn't show every extreme that they name: `owners`: each device's blocks name one owner at most 2 times; in every group some owner is named exactly 2 times by the blocks of every device of the group.
All inputs are finite; a program needn't handle non-finite values.
Results may differ from a plain program's by a relative error of at most 0.028.
Values may be sent and summed in bfloat16 or wider, within the bound.
A program may use at most 64 MiB of HBM per device.

v0:
```python
import math
import jax
import jax.numpy as jnp
from jax import lax
from jax.sharding import PartitionSpec as P

HEADS = 8


def token_pass(tokens, pooled, w_qk, w_in, w_out, pooled_grad):
    hidden_sum = tokens.astype(jnp.float32) + jnp.dot(
        pooled, w_in, preferred_element_type=jnp.float32
    )
    hidden = hidden_sum.astype(jnp.bfloat16)
    queries = jnp.dot(hidden, w_qk, preferred_element_type=jnp.float32).astype(jnp.bfloat16)
    num_rows = hidden.shape[0]
    head_cols = queries.shape[1]
    q_heads = queries.reshape(num_rows, HEADS, -1).astype(jnp.float32)
    score_scale = 1.0 / math.sqrt(q_heads.shape[2])
    scores = jnp.einsum("ihd,jhd->hij", q_heads, q_heads) * score_scale
    self_mask = jnp.eye(num_rows, dtype=bool)
    scores = jnp.where(self_mask[None], -1000000000.0, scores)
    row_max = jnp.max(scores, axis=2, keepdims=True)
    weights_exp = jnp.exp(scores - row_max)
    attn_prob = weights_exp / jnp.sum(weights_exp, axis=2, keepdims=True)
    prob_low = lax.optimization_barrier(attn_prob.astype(jnp.bfloat16)).astype(jnp.float32)
    hidden_wide = hidden.astype(jnp.float32)
    values = hidden_wide[:, :head_cols].reshape(num_rows, HEADS, -1)
    attended = jnp.einsum("hij,jhv->ihv", prob_low, values).reshape(num_rows, head_cols)
    output = jnp.concatenate(
        [hidden_wide[:, :head_cols] + attended, hidden_wide[:, head_cols:]], axis=1
    ).astype(jnp.bfloat16)
    unpooled = jnp.dot(output, w_out, preferred_element_type=jnp.float32).astype(jnp.bfloat16)
    out_grad = jnp.dot(pooled_grad, w_out.T, preferred_element_type=jnp.float32).astype(
        jnp.bfloat16
    )
    grad_heads = out_grad[:, :head_cols].reshape(num_rows, HEADS, -1).astype(jnp.float32)
    prob_grad = jnp.einsum("ihv,jhv->hij", grad_heads, values)
    score_grad = (
        attn_prob
        * (prob_grad - jnp.sum(prob_grad * attn_prob, axis=2, keepdims=True))
        * score_scale
    )
    score_low = lax.optimization_barrier(score_grad.astype(jnp.bfloat16)).astype(jnp.float32)
    q_grad = jnp.einsum("hij,jhd->ihd", score_low, q_heads) + jnp.einsum(
        "hji,jhd->ihd", score_low, q_heads
    )
    q_grad = q_grad.reshape(num_rows, -1).astype(jnp.bfloat16)
    return (unpooled, hidden, q_grad)


def local(tokens, w_qk, w_in, w_out, particles, cotangent, clusters, owners):
    n_shard = lax.axis_size("shard")
    num_blocks = owners.shape[0]
    block_rows = particles.shape[0] // num_blocks
    channels = particles.shape[1]
    capacity = 2 * num_blocks // n_shard
    slot_count = n_shard * capacity
    t_rows = tokens.shape[0]
    owner_hot = (owners[:, None] == jnp.arange(n_shard, dtype=jnp.int32)[None, :]).astype(jnp.int32)
    earlier = jnp.cumsum(owner_hot, axis=0) - owner_hot
    slot_rank = jnp.sum(earlier * owner_hot, axis=1)
    target = owners * capacity + slot_rank
    placing = (target[None, :] == jnp.arange(slot_count, dtype=jnp.int32)[:, None]).astype(
        jnp.bfloat16
    )
    feat_rows = particles.reshape(num_blocks, block_rows * channels)
    grad_rows = cotangent.reshape(num_blocks, block_rows * channels)
    send_feat = jnp.dot(placing, feat_rows, preferred_element_type=jnp.float32).astype(jnp.bfloat16)
    send_grad = jnp.dot(placing, grad_rows, preferred_element_type=jnp.float32).astype(jnp.bfloat16)
    label_rows = (clusters.reshape(num_blocks, block_rows) + 1).astype(jnp.float32)
    send_label = (
        jnp.dot(placing.astype(jnp.float32), label_rows, precision=lax.Precision.HIGHEST) - 1.0
    )
    send_feat = send_feat.reshape(n_shard, capacity, block_rows, channels)
    send_grad = send_grad.reshape(n_shard, capacity, block_rows, channels)
    send_label = send_label.astype(jnp.bfloat16).reshape(n_shard, capacity, block_rows)
    got_feat, got_grad, got_label = (
        lax.all_to_all(send_feat, "shard", split_axis=0, concat_axis=0, tiled=True),
        lax.all_to_all(send_grad, "shard", split_axis=0, concat_axis=0, tiled=True),
        lax.all_to_all(send_label, "shard", split_axis=0, concat_axis=0, tiled=True),
    )
    received = slot_count * block_rows
    labels = got_label.reshape(received).astype(jnp.float32)
    member = (labels[None, :] == jnp.arange(t_rows, dtype=jnp.float32)[:, None]).astype(
        jnp.bfloat16
    )
    counts = jnp.sum(member, axis=1, dtype=jnp.float32)
    pooled_sum = jnp.dot(
        member, got_feat.reshape(received, channels), preferred_element_type=jnp.float32
    )
    pooled = (pooled_sum / jnp.maximum(counts, 1.0)[:, None]).astype(jnp.bfloat16)
    pooled_grad = jnp.dot(
        member, got_grad.reshape(received, channels), preferred_element_type=jnp.float32
    ).astype(jnp.bfloat16)
    full_qk = lax.all_gather(w_qk, "shard", axis=0, tiled=True)
    unpooled, hidden, q_grad = token_pass(tokens, pooled, full_qk, w_in, w_out, pooled_grad)
    slot_values = jnp.einsum(
        "ts,tw->sw", member, unpooled, preferred_element_type=jnp.float32
    ).astype(jnp.bfloat16)
    slot_values = slot_values.reshape(n_shard, capacity, block_rows, channels)
    returned = lax.all_to_all(slot_values, "shard", split_axis=0, concat_axis=0, tiled=True)
    returned_rows = jnp.einsum(
        "sb,sx->bx",
        placing,
        returned.reshape(slot_count, block_rows * channels),
        preferred_element_type=jnp.float32,
    )
    returned_rows = returned_rows.reshape(num_blocks * block_rows, channels)
    particle_out = (particles.astype(jnp.float32) + returned_rows).astype(jnp.bfloat16)
    shard_sum = lax.psum_scatter(
        jnp.einsum("td,tk->dk", hidden, q_grad, preferred_element_type=jnp.float32).astype(
            jnp.bfloat16
        ),
        "shard",
        scatter_dimension=0,
        tiled=True,
    )
    qk_grad = lax.psum(shard_sum, "group").astype(jnp.float32)
    return (particle_out, qk_grad)


def solution(mesh):
    placed = (
        P(("group", "shard"), None),
        P("shard", None),
        P(),
        P(),
        P(("group", "shard"), None),
        P(("group", "shard"), None),
        P(("group", "shard")),
        P(("group", "shard")),
    )
    return jax.shard_map(
        local,
        mesh=mesh,
        in_specs=placed,
        out_specs=(P(("group", "shard"), None), P("shard", None)),
        check_vma=False,
    )
```

profile of v0, /device:TPU:8, one launch (start us, length us, event | category | flops | bytes accessed | tf_op | source)
XLA Modules:
  0.0 491.0 jit_solution(13615514162843825497)
XLA Ops:
  7.2 0.8 fusion.64
  8.0 0.8 select_reduce_fusion
  8.9 0.7 multiply_add_fusion
  9.5 1.5 fusion.22
  11.0 9.5 %all-to-all-start = ((bf16[32,2,128]{2,1,0:T(2,128)(2,1)}), bf16[32,2,128]{2,1,0:T(2,128)(2,1)S(1)}, u32[]{:S(2)}, u32[]{:S(2)}) async-start(bf16[32,2,128]{2,1,0:T(2,128)(2,1)} %bitcast.1), calls=%async_computation | async-start | bytes 32768 | tf_op jit(solution)/shard_map/all_to_all | solution.py:81
  20.5 1.5 reshape.76
  22.0 0.7 fusion.9
  22.7 1.9 copy.49
  24.6 2.9 all-to-all-done
  27.5 5.4 %all-to-all-start.1 = ((bf16[32,2,128,128]{3,2,1,0:T(8,128)(2,1)}), bf16[32,2,128,128]{3,2,1,0:T(8,128)(2,1)S(1)}, u32[]{:S(2)}, u32[]{:S(2)}) async-start(bf16[32,2,128,128]{3,2,1,0:T(8,128)(2,1)} %bitcast.79), calls=%async_computation.1 | async-start | bytes 4194304 | tf_op jit(solution)/shard_map/all_to_all | solution.py:79
  33.0 0.7 all-gather.2.cloned.1.call-update
  33.7 2.3 reshape.85
  36.0 1.9 fusion.10
  37.9 1.9 copy.51
  39.8 53.9 %all-to-all-done.1 = bf16[32,2,128,128]{3,2,1,0:T(8,128)(2,1)S(1)} async-done(((bf16[32,2,128,128]{3,2,1,0:T(8,128)(2,1)}), bf16[32,2,128,128]{3,2,1,0:T(8,128)(2,1)S(1)}, u32[]{:S(2)}, u32[]{:S(2)}) %all-to-all-start.1) | async-done | bytes 2097184 | tf_op jit(solution)/shard_map/all_to_all | solution.py:79
  93.6 5.6 %all-to-all-start.3 = ((bf16[32,2,128,128]{3,2,1,0:T(8,128)(2,1)}), bf16[32,2,128,128]{3,2,1,0:T(8,128)(2,1)}, u32[]{:S(2)}, u32[]{:S(2)}) async-start(bf16[32,2,128,128]{3,2,1,0:T(8,128)(2,1)} %bitcast.78), calls=%async_computation.3 | async-start | bytes 4194304 | tf_op jit(solution)/shard_map/all_to_all | solution.py:80
  99.3 0.3 convert_reduce_fusion
  99.7 1.6 fusion.2
  101.3 54.6 %all-to-all-done.3 = bf16[32,2,128,128]{3,2,1,0:T(8,128)(2,1)} async-done(((bf16[32,2,128,128]{3,2,1,0:T(8,128)(2,1)}), bf16[32,2,128,128]{3,2,1,0:T(8,128)(2,1)}, u32[]{:S(2)}, u32[]{:S(2)}) %all-to-all-start.3) | async-done | bytes 2097184 | tf_op jit(solution)/shard_map/all_to_all | solution.py:80
  155.9 2.3 fusion.25
  158.4 3.0 fusion.19
  161.4 0.3 fusion.77
  161.8 0.2 fusion.46
  162.2 3.2 convolution_convert_fusion.3
  165.8 1.3 convolution_convert_fusion.2
  167.1 62.9 %all_to_all.20 = bf16[32,2,128,128]{3,2,1,0:T(8,128)(2,1)S(1)} all-to-all(bf16[32,2,128,128]{3,2,1,0:T(8,128)(2,1)S(1)} %bitcast.80), channel_id=1, replica_groups=mesh['group'=16,'shard'=32] {'shard'}, dimensions={0} | all-to-all | bytes 4194304 | tf_op jit(solution)/shard_map/all_to_all | solution.py:102
  230.0 2.8 fusion.3
  232.8 1.7 reshape.84
  234.6 63.5 %reduce-scatter.2.cloned.1.call-done = bf16[64,1024]{1,0:T(8,128)(2,1)} async-done(((bf16[2048,1024]{1,0:T(8,128)(2,1)}), bf16[64,1024]{1,0:T(8,128)(2,1)}) %reduce-scatter.2.cloned.1.call-update) | async-done | bytes 131088 | tf_op jit(solution)/shard_map/reduce_scatter | solution.py:111
  298.1 2.4 add_convert_fusion
  300.5 182.3 %all-reduce.2.cloned.1.call-done = bf16[64,1024]{1,0:T(8,128)(2,1)} async-done(((bf16[64,1024]{1,0:T(8,128)(2,1)}), bf16[64,1024]{1,0:T(8,128)(2,1)}) %all-reduce.2.cloned.1.call-update) | async-done | bytes 131088 | tf_op jit(solution)/shard_map/psum | solution.py:119
  482.9 1.6 convert_element_type.119
  (21 shorter events, 1.0 us)
Async XLA Ops:
  7.2 148.7 %copy-start = (bf16[2048,128]{1,0:T(8,128)(2,1)S(1)}, bf16[2048,128]{1,0:T(8,128)(2,1)}, u32[]{:S(2)}) copy-start(bf16[2048,128]{1,0:T(8,128)(2,1)} %param.11) | copy-start | bytes 1572868
  11.0 16.5 %all-to-all-start = ((bf16[32,2,128]{2,1,0:T(2,128)(2,1)}), bf16[32,2,128]{2,1,0:T(2,128)(2,1)S(1)}, u32[]{:S(2)}, u32[]{:S(2)}) async-start(bf16[32,2,128]{2,1,0:T(2,128)(2,1)} %bitcast.1), calls=%async_computation | async-start | bytes 32768 | tf_op jit(solution)/shard_map/all_to_all | solution.py:81
  27.5 66.1 %all-to-all-start.1 = ((bf16[32,2,128,128]{3,2,1,0:T(8,128)(2,1)}), bf16[32,2,128,128]{3,2,1,0:T(8,128)(2,1)S(1)}, u32[]{:S(2)}, u32[]{:S(2)}) async-start(bf16[32,2,128,128]{3,2,1,0:T(8,128)(2,1)} %bitcast.79), calls=%async_computation.1 | async-start | bytes 4194304 | tf_op jit(solution)/shard_map/all_to_all | solution.py:79
  32.9 125.5 %all-gather.2.cloned.1.call-start = ((), (), s32[]{:S(2)}) async-start(), calls=%async_computation.5 | async-start | bytes 4325376 | tf_op jit(solution)/shard_map/all_gather | solution.py:96
  93.6 6.0 %copy-start.1 = (bf16[128,2048]{1,0:T(8,128)(2,1)S(1)}, bf16[128,2048]{1,0:T(8,128)(2,1)}, u32[]{:S(2)}) copy-start(bf16[128,2048]{1,0:T(8,128)(2,1)} %param.10) | copy-start | bytes 1572868
  93.6 62.2 %all-to-all-start.3 = ((bf16[32,2,128,128]{3,2,1,0:T(8,128)(2,1)}), bf16[32,2,128,128]{3,2,1,0:T(8,128)(2,1)}, u32[]{:S(2)}, u32[]{:S(2)}) async-start(bf16[32,2,128,128]{3,2,1,0:T(8,128)(2,1)} %bitcast.78), calls=%async_computation.3 | async-start | bytes 4194304 | tf_op jit(solution)/shard_map/all_to_all | solution.py:80
  99.3 198.8 %reduce-scatter.2.cloned.1.call-start = ((), (), s32[]{:S(2)}) async-start(), calls=%async_computation.6 | async-start | bytes 4325376 | tf_op jit(solution)/shard_map/reduce_scatter | solution.py:111
  165.4 317.4 %all-reduce.2.cloned.1.call-start = ((), (), s32[]{:S(2)}) async-start(), calls=%async_computation.7 | async-start | bytes 262144 | tf_op jit(solution)/shard_map/psum | solution.py:119
Sparse Core Ops, SparseCore 0:
  35.9 94.9 all-gather.1
  165.6 132.5 reduce-scatter.1
  301.0 181.8 all-reduce.1
where the time goes:
time: 492 us; the launch traced here: 491 us
  waiting for transfers between devices  358 us (73%)
  blocking collectives  62.9 us (13%)
  starting transfers between devices  20.6 us (4%)
  matrix products  19.4 us (4%)
  between operations  13.9 us (3%)
  local copies, waits for them, and re-layouts  9.43 us (2%)
  other arithmetic  6.86 us (1%)
    psum x1, waiting for transfers between devices, local(): qk_grad = lax.psum(shard_sum, 'group').astype(jnp.float32)  182 us
    reduce_scatter x1, waiting for transfers between devices, local(): lax.psum_scatter(jnp.einsum('td,tk->dk', hidden, q_grad, preferred_elemen...  63.5 us
    all_to_all x1, blocking collectives, local(): lax.all_to_all(slot_values, 'shard', split_axis=0, concat_axis=0, tiled=T...  62.9 us
    all_to_all x1, waiting for transfers between devices, local(): lax.all_to_all(send_grad, 'shard', split_axis=0, concat_axis=0, tiled=True)  54.6 us
    all_to_all x1, waiting for transfers between devices, local(): lax.all_to_all(send_feat, 'shard', split_axis=0, concat_axis=0, tiled=True)  53.9 us
  transfers between devices with their start and end apart: 6, of which 5 were waited for; matrix products, arithmetic and copies ran while one was open for 5% of the time, Pallas kernels for 0%

commit v1 on v0

--- a/solution.py
+++ b/solution.py
@@ -116,7 +116,7 @@
         scatter_dimension=0,
         tiled=True,
     )
-    qk_grad = lax.psum(shard_sum, "group").astype(jnp.float32)
+    qk_grad = jnp.sum(lax.all_gather(shard_sum, "group"), axis=0).astype(jnp.float32)
     return (particle_out, qk_grad)
 
 

time: 492 us -> 386 us (0.78)
  blocking collectives: 62.9 us -> 0 us
  waiting for transfers between devices: 358 us -> 308 us
    psum x1 -> x0, waiting for transfers between devices: 182 us -> none  [local(): qk_grad = lax.psum(shard_sum, 'group').astype(jnp.float32)]
    all_gather x0 -> x1, waiting for transfers between devices: none -> 69 us  [local(): lax.all_gather(shard_sum, 'group')]
    reduce_scatter x1, waiting for transfers between devices: 63.5 us -> 127 us  [local(): lax.psum_scatter(jnp.einsum('td,tk->dk', hidden, q_grad, preferred_elemen...]
    all_to_all x1 -> x0, blocking collectives: 62.9 us -> none  [local(): lax.all_to_all(slot_values, 'shard', split_axis=0, concat_axis=0, tiled=T...]
  transfers between devices with their start and end apart: 6 -> 7, of which waited for: 5 -> 5; matrix products, arithmetic and copies ran while one was open for 5% -> 6% of each run, Pallas kernels for 0% -> 0%
where the time goes in v1:
time: 386 us; the launch traced here: 385 us
  waiting for transfers between devices  308 us (80%)
  starting transfers between devices  25.5 us (7%)
  matrix products  20.7 us (5%)
  between operations  13.9 us (4%)
  local copies, waits for them, and re-layouts  9.41 us (2%)
  other arithmetic  7.93 us (2%)
    reduce_scatter x1, waiting for transfers between devices, local(): lax.psum_scatter(jnp.einsum('td,tk->dk', hidden, q_grad, preferred_elemen...  127 us
    all_gather x1, waiting for transfers between devices, local(): lax.all_gather(shard_sum, 'group')  69 us
    all_to_all x1, waiting for transfers between devices, local(): lax.all_to_all(send_grad, 'shard', split_axis=0, concat_axis=0, tiled=True)  54.6 us
    all_to_all x1, waiting for transfers between devices, local(): lax.all_to_all(send_feat, 'shard', split_axis=0, concat_axis=0, tiled=True)  53.9 us
    all_to_all x1, starting transfers between devices, local(): lax.all_to_all(send_label, 'shard', split_axis=0, concat_axis=0, tiled=True)  9.51 us
  transfers between devices with their start and end apart: 7, of which 5 were waited for; matrix products, arithmetic and copies ran while one was open for 6% of the time, Pallas kernels for 0%

profile of v1, /device:TPU:8, one launch (start us, length us, event | category | flops | bytes accessed | tf_op | source)
XLA Modules:
  0.0 385.5 jit_solution(12822318046470879535)
XLA Ops:
  7.2 0.8 fusion.64
  8.0 0.8 select_reduce_fusion
  8.9 0.7 multiply_add_fusion
  9.5 1.5 fusion.22
  11.0 9.5 %all-to-all-start = ((bf16[32,2,128]{2,1,0:T(2,128)(2,1)}), bf16[32,2,128]{2,1,0:T(2,128)(2,1)S(1)}, u32[]{:S(2)}, u32[]{:S(2)}) async-start(bf16[32,2,128]{2,1,0:T(2,128)(2,1)} %bitcast.1), calls=%async_computation | async-start | bytes 32768 | tf_op jit(solution)/shard_map/all_to_all | solution.py:81
  20.5 1.5 reshape.76
  22.0 0.7 fusion.9
  22.7 1.9 copy.49
  24.6 2.9 all-to-all-done
  27.5 5.4 %all-to-all-start.1 = ((bf16[32,2,128,128]{3,2,1,0:T(8,128)(2,1)}), bf16[32,2,128,128]{3,2,1,0:T(8,128)(2,1)S(1)}, u32[]{:S(2)}, u32[]{:S(2)}) async-start(bf16[32,2,128,128]{3,2,1,0:T(8,128)(2,1)} %bitcast.81), calls=%async_computation.1 | async-start | bytes 4194304 | tf_op jit(solution)/shard_map/all_to_all | solution.py:79
  33.0 0.7 all-gather.4.cloned.1.call-update
  33.7 2.3 reshape.85
  36.0 1.9 fusion.10
  37.9 1.9 copy.51
  39.8 53.9 %all-to-all-done.1 = bf16[32,2,128,128]{3,2,1,0:T(8,128)(2,1)S(1)} async-done(((bf16[32,2,128,128]{3,2,1,0:T(8,128)(2,1)}), bf16[32,2,128,128]{3,2,1,0:T(8,128)(2,1)S(1)}, u32[]{:S(2)}, u32[]{:S(2)}) %all-to-all-start.1) | async-done | bytes 2097184 | tf_op jit(solution)/shard_map/all_to_all | solution.py:79
  93.6 5.6 %all-to-all-start.3 = ((bf16[32,2,128,128]{3,2,1,0:T(8,128)(2,1)}), bf16[32,2,128,128]{3,2,1,0:T(8,128)(2,1)}, u32[]{:S(2)}, u32[]{:S(2)}) async-start(bf16[32,2,128,128]{3,2,1,0:T(8,128)(2,1)} %bitcast.79), calls=%async_computation.3 | async-start | bytes 4194304 | tf_op jit(solution)/shard_map/all_to_all | solution.py:80
  99.3 0.3 convert_reduce_fusion
  99.7 1.6 fusion.2
  101.3 54.6 %all-to-all-done.3 = bf16[32,2,128,128]{3,2,1,0:T(8,128)(2,1)} async-done(((bf16[32,2,128,128]{3,2,1,0:T(8,128)(2,1)}), bf16[32,2,128,128]{3,2,1,0:T(8,128)(2,1)}, u32[]{:S(2)}, u32[]{:S(2)}) %all-to-all-start.3) | async-done | bytes 2097184 | tf_op jit(solution)/shard_map/all_to_all | solution.py:80
  155.9 2.3 fusion.25
  158.4 3.0 fusion.19
  161.4 0.3 fusion.77
  162.2 3.2 convolution_convert_fusion.3
  165.7 2.6 convolution_convert_fusion.2
  168.4 4.9 %all-to-all-start.2 = ((bf16[32,2,128,128]{3,2,1,0:T(8,128)(2,1)}), bf16[32,2,128,128]{3,2,1,0:T(8,128)(2,1)S(1)}, u32[]{:S(2)}, u32[]{:S(2)}) async-start(bf16[32,2,128,128]{3,2,1,0:T(8,128)(2,1)} %bitcast.82), calls=%async_computation.2 | async-start | bytes 4194304 | tf_op jit(solution)/shard_map/all_to_all | solution.py:102
  173.3 127.0 %reduce-scatter.2.cloned.1.call-done = bf16[64,1024]{1,0:T(8,128)(2,1)} async-done(((bf16[2048,1024]{1,0:T(8,128)(2,1)}), bf16[64,1024]{1,0:T(8,128)(2,1)}) %reduce-scatter.2.cloned.1.call-update) | async-done | bytes 131088 | tf_op jit(solution)/shard_map/reduce_scatter | solution.py:111
  300.4 2.8 fusion.3
  303.1 1.7 reshape.84
  304.9 2.4 add_convert_fusion
  307.3 69.0 %all-gather.6.cloned.1.call-done = bf16[1024,1024]{1,0:T(8,128)(2,1)} async-done(((bf16[64,1024]{1,0:T(8,128)(2,1)}), bf16[1024,1024]{1,0:T(8,128)(2,1)}) %all-gather.6.cloned.1.call-update) | async-done | bytes 2097168 | tf_op jit(solution)/shard_map/all_gather | solution.py:119
  376.2 2.0 reduce_sum.52
  378.2 0.7 convert_element_type.121
  (23 shorter events, 1.2 us)
Async XLA Ops:
  7.2 148.7 %copy-start = (bf16[2048,128]{1,0:T(8,128)(2,1)S(1)}, bf16[2048,128]{1,0:T(8,128)(2,1)}, u32[]{:S(2)}) copy-start(bf16[2048,128]{1,0:T(8,128)(2,1)} %param.11) | copy-start | bytes 1572868
  11.0 16.5 %all-to-all-start = ((bf16[32,2,128]{2,1,0:T(2,128)(2,1)}), bf16[32,2,128]{2,1,0:T(2,128)(2,1)S(1)}, u32[]{:S(2)}, u32[]{:S(2)}) async-start(bf16[32,2,128]{2,1,0:T(2,128)(2,1)} %bitcast.1), calls=%async_computation | async-start | bytes 32768 | tf_op jit(solution)/shard_map/all_to_all | solution.py:81
  27.5 66.1 %all-to-all-start.1 = ((bf16[32,2,128,128]{3,2,1,0:T(8,128)(2,1)}), bf16[32,2,128,128]{3,2,1,0:T(8,128)(2,1)S(1)}, u32[]{:S(2)}, u32[]{:S(2)}) async-start(bf16[32,2,128,128]{3,2,1,0:T(8,128)(2,1)} %bitcast.81), calls=%async_computation.1 | async-start | bytes 4194304 | tf_op jit(solution)/shard_map/all_to_all | solution.py:79
  32.9 125.5 %all-gather.4.cloned.1.call-start = ((), (), s32[]{:S(2)}) async-start(), calls=%async_computation.5 | async-start | bytes 4325376 | tf_op jit(solution)/shard_map/all_gather | solution.py:96
  93.6 6.0 %copy-start.1 = (bf16[128,2048]{1,0:T(8,128)(2,1)S(1)}, bf16[128,2048]{1,0:T(8,128)(2,1)}, u32[]{:S(2)}) copy-start(bf16[128,2048]{1,0:T(8,128)(2,1)} %param.10) | copy-start | bytes 1572868
  93.6 62.2 %all-to-all-start.3 = ((bf16[32,2,128,128]{3,2,1,0:T(8,128)(2,1)}), bf16[32,2,128,128]{3,2,1,0:T(8,128)(2,1)}, u32[]{:S(2)}, u32[]{:S(2)}) async-start(bf16[32,2,128,128]{3,2,1,0:T(8,128)(2,1)} %bitcast.79), calls=%async_computation.3 | async-start | bytes 4194304 | tf_op jit(solution)/shard_map/all_to_all | solution.py:80
  99.3 201.1 %reduce-scatter.2.cloned.1.call-start = ((), (), s32[]{:S(2)}) async-start(), calls=%async_computation.6 | async-start | bytes 4325376 | tf_op jit(solution)/shard_map/reduce_scatter | solution.py:111
  168.4 132.0 %all-to-all-start.2 = ((bf16[32,2,128,128]{3,2,1,0:T(8,128)(2,1)}), bf16[32,2,128,128]{3,2,1,0:T(8,128)(2,1)S(1)}, u32[]{:S(2)}, u32[]{:S(2)}) async-start(bf16[32,2,128,128]{3,2,1,0:T(8,128)(2,1)} %bitcast.82), calls=%async_computation.2 | async-start | bytes 4194304 | tf_op jit(solution)/shard_map/all_to_all | solution.py:102
  173.3 202.9 %all-gather.6.cloned.1.call-start = ((), (), s32[]{:S(2)}) async-start(), calls=%async_computation.7 | async-start | bytes 2228224 | tf_op jit(solution)/shard_map/all_gather | solution.py:119
Sparse Core Ops, SparseCore 0:
  35.9 94.9 all-gather.3
  165.5 134.7 reduce-scatter.1
  303.4 72.8 all-gather.5
